TPU v7x, 32 devices: a whole 2x2x4 slice. The times are simulated.
32 devices in a mesh: groups: 2 (over x), ctx: 16 (over z, y, core).
Axes of the slice: x: 2, y: 2, z: 4, core: 2. Of those that a mesh axis runs over, the one named last changes fastest.
Arguments:
- query_input: bfloat16 [32, 1536], P('groups'), parts along dimension 0, may hold values from -20 to 20
- query_gain: bfloat16 [1536], replicated, may hold values from 0.5 to 1.5
- nope_weight: bfloat16 [1536, 4096], P(None, 'ctx'), may hold values from -0.15625 to 0.15625
- rope_weight: bfloat16 [1536, 2048], P(None, 'ctx'), may hold values from -0.15625 to 0.15625
- key_up: bfloat16 [32, 128, 512], P('ctx'), may hold values from -0.5 to 0.5
- value_up: bfloat16 [32, 512, 128], P('ctx'), may hold values from -1 to 1
- out_weight: bfloat16 [4096, 7168], P('ctx'), may hold values from -0.09375 to 0.09375
- cache_latent: bfloat16 [4, 32768, 512], P('groups', 'ctx'), parts along dimension 0, may hold values from -8 to 8
- cache_rope: bfloat16 [4, 64, 32768], P('groups', None, 'ctx'), parts along dimension 0, may hold values from -256 to 256
- cached_length: int32 [4], P('groups'), parts along dimension 0, may hold values from 16384 to 32760, as said below
Outputs:
- attn_out: bfloat16 [32, 7168], P('groups'), parts along dimension 0
There are 2 independent parts, one for each index of `groups`. A program takes and returns all parts, laid end to end along the dimension named above; an argument that names none is the same for every part. Nothing has to cross between parts.
Inputs may be any that keep to these rules, and one draw needn't show every extreme that they name: `cached_length`: in every part one request has exactly 32760, so that its last new token sees the cache's last position.
All inputs are finite; a program needn't handle non-finite values.
Results may differ from a plain program's by a relative error of at most 0.012.
Values may be sent and summed in bfloat16 or wider, within the bound.
A program may use at most 128 MiB of HBM per device.

v0:
```python
import functools
import math

import jax
import jax.numpy as jnp
from jax import lax
from jax.experimental import pallas as pl
from jax.experimental.pallas import tpu as pltpu
from jax.sharding import PartitionSpec as P

mscale_yarn = 1.0 + 0.1 * math.log(40.0)
masked_score = -1e30
MESH = pl.DeviceIdType.MESH
F32 = jnp.float32
BF16 = jnp.bfloat16
NT = (((1,), (1,)), ((), ()))


def kernel(
    n, tile,
    x_hbm, gain_ref, nope_hbm, ropew_hbm, kup_hbm, vup_hbm, outw_hbm, lat_hbm, crope_hbm, len_ref,
    out_ref,
    x_v, nope_v, ropew_v, kup_v, vup_v, outw_v, lat_v, crope_v,
    qbuf, score_s, peak_s, sum_s, pool_s, pk_buf, sm_buf,
    sb1, rb1, sb2, rb2,
    opart, ob1, or1, os2, or2, fin,
    ld_sem,
    q1s, q1r, q2s, q2r,
    pks, pkr, sms, smr,
    p1s, p1r, p2s, p2r,
    o1s, o1r, o2s, o2r,
    f1s, f1r, f2s, f2r,
):
    me = lax.axis_index("ctx")
    chips = n // 2
    chip, c = me // 2, me % 2
    heads, nope_w, lat_w = kup_v.shape
    rows = x_v.shape[0]
    requests, keys, _ = lat_v.shape
    model = out_ref.shape[1]
    stretch = rows // requests
    block_rows = heads * stretch
    rope_all = ropew_v.shape[1]
    rope_w = rope_all // heads
    scale = mscale_yarn * mscale_yarn / math.sqrt(nope_w + rope_w)

    def peer(k):
        flipped, bit = 0, 1
        while bit < chips:
            flipped = flipped + ((chip // bit + (k // bit) % 2) % 2) * bit
            bit *= 2
        return flipped

    near_first = sorted(range(1, chips), key=lambda k: (bin(k).count("1"), k))
    order = near_first + [0]

    def remote(src, dst, ssem, rsem, target):
        return pltpu.make_async_remote_copy(
            src_ref=src, dst_ref=dst, send_sem=ssem, recv_sem=rsem,
            device_id={"ctx": target}, device_id_type=MESH,
        )

    loads = []

    def load(src, dst):
        copy = pltpu.make_async_copy(src, dst, ld_sem.at[len(loads)])
        copy.start()
        loads.append(copy)
        return copy

    load_x = load(x_hbm, x_v)
    load_nope = load(nope_hbm, nope_v)
    load_rope = load(ropew_hbm, ropew_v)
    load_kup = load(kup_hbm, kup_v)
    barrier = pltpu.get_barrier_semaphore()
    for k in range(1, n):
        pl.semaphore_signal(
            barrier, inc=1, device_id={"ctx": (me + k) % n}, device_id_type=MESH
        )

    load_x.wait()
    widened = x_v[...].astype(F32)
    normed = (
        widened
        * lax.rsqrt(jnp.mean(widened * widened, axis=-1, keepdims=True) + 1e-06)
        * gain_ref[...].astype(F32).reshape(1, -1)
    ).astype(BF16)
    load_nope.wait()
    query_nope = jnp.dot(normed, nope_v[...], preferred_element_type=F32).astype(BF16)
    load_rope.wait()
    query_rope = jnp.dot(normed, ropew_v[...], preferred_element_type=F32)
    load_kup.wait()
    load_cache = [load(lat_hbm, lat_v)]
    for h in range(heads):
        load_cache.append(load(crope_hbm, crope_v.at[:, h * rope_w : (h + 1) * rope_w, :]))
    load_vup = load(vup_hbm, vup_v)
    load_outw = load(outw_hbm, outw_v.at[:, :model])
    if outw_v.shape[1] > model:
        outw_v[:, model:] = jnp.zeros((outw_v.shape[0], outw_v.shape[1] - model), BF16)
    latents = [
        jnp.dot(
            query_nope[:, h * nope_w : (h + 1) * nope_w], kup_v[h], preferred_element_type=F32
        )
        for h in range(heads)
    ]
    lane_head = lax.broadcasted_iota(jnp.int32, (stretch, rope_all), 1) // rope_w
    for b in range(requests):
        part = slice(b * stretch, (b + 1) * stretch)
        qbuf[me, b, :, :lat_w] = jnp.concatenate([t[part] for t in latents], axis=0).astype(BF16)
        qbuf[me, b, :, lat_w:] = jnp.concatenate(
            [jnp.where(lane_head == h, query_rope[part], 0.0) for h in range(heads)], axis=0
        ).astype(BF16)
    pl.semaphore_wait(barrier, n - 1)

    pending = []

    def send(copy):
        copy.start()
        pending.append(copy)

    def gather(at, s1, r1, s2, r2):
        def to_chip(k, source):
            ref = at(source, c)
            return remote(ref, ref, s1.at[k], r1.at[k], peer(k) * 2 + c)

        def to_core(k, side):
            ref = at(peer(k), side)
            return remote(ref, ref, s2.at[k], r2.at[k], chip * 2 + 1 - c)

        for k in near_first:
            send(to_chip(k, chip))
        send(to_core(0, c))
        for k in near_first:
            to_chip(k, peer(k)).wait_recv()
            send(to_core(k, c))
        for k in range(chips):
            to_core(k, 1 - c).wait_recv()

    gather(lambda at_chip, side: qbuf.at[at_chip * 2 + side], q1s, q1r, q2s, q2r)

    for copy in load_cache:
        copy.wait()
    first_key = me * keys
    tile_devs = tile // block_rows
    tiles_per = n // tile_devs
    tiles = requests * tiles_per

    def each_tile(body):
        if tiles <= 2:
            for t in range(tiles):
                body(t, t // tiles_per, (t % tiles_per) * tile_devs, t * tile)
        else:
            def step(t, carry):
                body(
                    t, t // tiles_per, (t % tiles_per) * tile_devs,
                    pl.multiple_of(t * tile, tile),
                )
                return carry
            lax.fori_loop(0, tiles, step, 0)

    def compact(column):
        return jnp.transpose(jnp.broadcast_to(column, (tile, 128)))[0:1, :]

    def spread(row):
        return jnp.transpose(jnp.broadcast_to(row, (128, tile)))[:, 0:1]

    def scores_of(t, b, d0, r0):
        query = qbuf[pl.ds(d0, tile_devs), b].reshape(tile, lat_w + rope_all)
        raw = lax.dot_general(query[:, :lat_w], lat_v[b], NT, preferred_element_type=F32)
        raw = raw + jnp.dot(query[:, lat_w:], crope_v[b], preferred_element_type=F32)
        row = lax.broadcasted_iota(jnp.int32, (tile, 1), 0) % stretch
        limit = len_ref[b] + row - first_key
        where_key = lax.broadcasted_iota(jnp.int32, (tile, keys), 1)
        raw = jnp.where(where_key <= limit, raw, masked_score)
        score_s[t] = raw
        peak = jnp.max(raw, axis=1, keepdims=True)
        peak_s[pl.ds(r0, tile), :] = jnp.broadcast_to(peak, (tile, 128))
        pk_buf[me, :, pl.ds(r0, tile)] = compact(peak)

    each_tile(scores_of)

    def share(buf, ss, rs):
        for k in range(1, n):
            send(remote(buf.at[me], buf.at[me], ss.at[k], rs.at[k], (me + k) % n))

    def shared(buf, ss, rs):
        for k in range(1, n):
            ref = buf.at[(me + n - k) % n]
            remote(ref, ref, ss.at[k], rs.at[k], (me + k) % n).wait_recv()

    share(pk_buf, pks, pkr)

    def pool_of(t, b, d0, r0):
        peak = peak_s[pl.ds(r0, tile), 0:1]
        weights = jnp.exp((score_s[t] - peak) * scale)
        sum_s[pl.ds(r0, tile), :] = jnp.broadcast_to(
            jnp.sum(weights, axis=1, keepdims=True), (tile, 128)
        )
        pool_s[b, pl.ds(d0, tile_devs)] = jnp.dot(
            weights.astype(BF16), lat_v[b], preferred_element_type=F32
        ).reshape(tile_devs, block_rows, lat_w)

    each_tile(pool_of)
    shared(pk_buf, pks, pkr)

    def rescale(t, b, d0, r0):
        top = jnp.max(pk_buf[:, :, pl.ds(r0, tile)], axis=0)
        factor = jnp.exp((peak_s[pl.ds(r0, tile), 0:1] - spread(top)) * scale)
        sm_buf[me, :, pl.ds(r0, tile)] = compact(sum_s[pl.ds(r0, tile), 0:1] * factor)
        scaled = pool_s[b, pl.ds(d0, tile_devs)].reshape(tile, lat_w) * factor
        scaled = scaled.reshape(tile_devs, block_rows, lat_w)
        pool_s[b, pl.ds(d0, tile_devs)] = scaled
        sb1[pl.ds(d0, tile_devs), b] = scaled.astype(BF16)

    each_tile(rescale)

    def to_core(k):
        return remote(
            sb1.at[peer(k) * 2 + 1 - c], rb1.at[k], p1s.at[k], p1r.at[k], chip * 2 + 1 - c
        )

    def to_chip(k):
        return remote(sb2.at[k], rb2.at[k], p2s.at[k], p2r.at[k], peer(k) * 2 + c)

    for k in order:
        send(to_core(k))
    share(sm_buf, sms, smr)
    for k in order:
        to_core(k).wait_recv()
        total = pool_s[:, peer(k) * 2 + c] + rb1[k].astype(F32)
        if k:
            sb2[k] = total.astype(BF16)
            send(to_chip(k))
    for k in range(1, chips):
        to_chip(k).wait_recv()
        total = total + rb2[k].astype(F32)
    shared(sm_buf, sms, smr)

    all_sums = jnp.sum(sm_buf[...], axis=0)
    per_request = n * block_rows
    owner = lax.broadcasted_iota(jnp.int32, (block_rows, per_request), 1)
    mine = owner == me * block_rows + lax.broadcasted_iota(
        jnp.int32, (block_rows, per_request), 0
    )
    attended = []
    for b in range(requests):
        sums = jnp.sum(
            jnp.where(mine, all_sums[:, b * per_request : (b + 1) * per_request], 0.0),
            axis=1, keepdims=True,
        )
        attended.append(total[b] / sums)
    load_vup.wait()
    values = []
    for h in range(heads):
        stacked = jnp.concatenate(
            [t[h * stretch : (h + 1) * stretch] for t in attended], axis=0
        ).astype(BF16)
        values.append(jnp.dot(stacked, vup_v[h], preferred_element_type=F32).astype(BF16))
    head_values = jnp.concatenate(values, axis=1)

    half = rows // 2
    width = opart.shape[3]

    def to_core_out(k):
        return remote(ob1.at[k, 1 - c], or1.at[k], o1s.at[k], o1r.at[k], chip * 2 + 1 - c)

    def to_chip_out(k):
        return remote(os2.at[k], or2.at[k], o2s.at[k], o2r.at[k], peer(k) * 2 + c)

    def pair_out(k):
        to_core_out(k).wait_recv()
        summed = opart[k, c] + or1[k].astype(F32)
        if k:
            os2[k] = summed.astype(BF16)
            send(to_chip_out(k))
        return summed

    load_outw.wait()
    lag = min(2, chips - 1)
    for i, k in enumerate(order):
        columns = pl.ds(pl.multiple_of(peer(k) * width, 128), width)
        partial = jnp.dot(head_values, outw_v[:, columns], preferred_element_type=F32)
        for side in range(2):
            piece = partial[side * half : (side + 1) * half]
            opart[k, side] = piece
            ob1[k, side] = piece.astype(BF16)
        send(to_core_out(k))
        if i >= lag:
            pair_out(order[i - lag])
    for k in order[chips - lag :]:
        summed = pair_out(k)
    for k in range(1, chips):
        to_chip_out(k).wait_recv()
        summed = summed + or2[k].astype(F32)
    fin[chip, c] = summed.astype(BF16)
    gather(lambda at_chip, side: fin.at[at_chip, side], f1s, f1r, f2s, f2r)

    for q in range(chips):
        used = max(0, min(width, model - q * width))
        if used:
            out_ref[:, q * width : q * width + used] = jnp.concatenate(
                [fin[q, 0, :, :used].astype(F32), fin[q, 1, :, :used].astype(F32)], axis=0
            ).astype(BF16)
    for copy in pending:
        copy.wait_send()


def local(
    n, query_input, query_gain, nope_weight, rope_weight, key_up, value_up, out_weight,
    cache_latent, cache_rope, cached_length,
):
    heads, nope_w, lat_w = key_up.shape
    rows = query_input.shape[0]
    requests, keys, _ = cache_latent.shape
    stretch = rows // requests
    block_rows = heads * stretch
    rope_all = rope_weight.shape[1]
    rope_w = rope_all // heads
    model = out_weight.shape[1]
    chips = n // 2
    flat = requests * n * block_rows
    tile = min(256, n * block_rows)
    half = rows // 2
    lane_tiles = -(-model // 128)
    width = -(-lane_tiles // chips) * 128
    block = (requests, block_rows, lat_w)
    vmem = pltpu.VMEM
    dma = lambda count: pltpu.SemaphoreType.DMA((count,))
    any_spec = pl.BlockSpec(memory_space=pl.ANY)
    vmem_spec = pl.BlockSpec(memory_space=pltpu.VMEM)
    sems = [dma(chips)] * 4
    return pl.pallas_call(
        functools.partial(kernel, n, tile),
        out_shape=jax.ShapeDtypeStruct((rows, model), BF16),
        in_specs=[any_spec, vmem_spec] + [any_spec] * 7
        + [pl.BlockSpec(memory_space=pltpu.SMEM)],
        out_specs=vmem_spec,
        scratch_shapes=[
            vmem(query_input.shape, BF16), vmem(nope_weight.shape, BF16),
            vmem(rope_weight.shape, BF16), vmem(key_up.shape, BF16),
            vmem(value_up.shape, BF16), vmem((out_weight.shape[0], chips * width), BF16),
            vmem(cache_latent.shape, BF16), vmem((requests, rope_all, keys), BF16),
            vmem((n, requests, block_rows, lat_w + rope_all), BF16),
            vmem((flat // tile, tile, keys), F32),
            vmem((flat, 128), F32), vmem((flat, 128), F32),
            vmem((requests, n, block_rows, lat_w), F32),
            vmem((n, 1, flat), F32), vmem((n, 1, flat), F32),
            vmem((n, *block), BF16), vmem((chips, *block), BF16),
            vmem((chips, *block), BF16), vmem((chips, *block), BF16),
            vmem((chips, 2, half, width), F32), vmem((chips, 2, half, width), BF16),
            vmem((chips, half, width), BF16), vmem((chips, half, width), BF16),
            vmem((chips, half, width), BF16), vmem((chips, 2, half, width), BF16),
            dma(7 + heads),
            *sems, dma(n), dma(n), dma(n), dma(n), *sems, *sems, *sems,
        ],
        compiler_params=pltpu.CompilerParams(
            collective_id=0, has_side_effects=True, vmem_limit_bytes=63 * 1024 * 1024
        ),
    )(
        query_input, query_gain, nope_weight, rope_weight, key_up,
        value_up, out_weight, cache_latent, cache_rope, cached_length,
    )


def solution(mesh):
    placed = (
        P("groups", None),
        P(),
        P(None, "ctx"),
        P(None, "ctx"),
        P("ctx", None, None),
        P("ctx", None, None),
        P("ctx", None),
        P("groups", "ctx", None),
        P("groups", None, "ctx"),
        P("groups"),
    )
    return jax.shard_map(
        functools.partial(local, mesh.shape["ctx"]), mesh=mesh, in_specs=placed,
        out_specs=P("groups", None), check_vma=False,
    )
```

profile of v0, /device:TPU:0, one launch (start us, length us, event | category | flops | bytes accessed | tf_op | source)
XLA Modules:
  0.0 48.4 jit_solution(14687759540168762482)
XLA Ops:
  0.0 46.8 %shard_map.100 = bf16[16,7168]{1,0:T(8,128)(2,1)} custom-call(bf16[16,1536]{1,0:T(8,128)(2,1)} %x_hbm.1, bf16[1536]{0:T(1024)(128)(2,1)} %gain_ref.1, bf16[1536,256]{1,0:T(8,128)(2,1)} %nope_hbm.1, bf16[1536,128]{1,0:T(8,128)(2,1)} %ropew_hbm.1, bf16[2,128,512]{2,1,0:T(8,128)(2,1)} %kup_hbm.1, bf16[2,512,128]{2,1,0:T(8,128)(2,1)} %vup_hbm.1, ...), custom_call_target="tpu_custom_call" | custom-call | tf_op jit(solution)/shard_map/pallas_call | solution.py:332
  46.8 1.6 %copy.12 = bf16[16,7168]{1,0:T(8,128)(2,1)} copy(bf16[16,7168]{1,0:T(8,128)(2,1)} %shard_map.100) | data formatting | bytes 458752
where the time goes:
time: 48.6 us; the launch traced here: 48.4 us
  Pallas kernels  46.8 us (96%)
  local copies, waits for them, and re-layouts  1.64 us (3%)
    pallas_call x1, Pallas kernels, local(): pl.pallas_call(functools.partial(kernel, n, tile), out_shape=jax.ShapeDty...  46.8 us
    unnamed x1, local copies, waits for them, and re-layouts  1.64 us

commit v1 on v0

v1 whole, which is shorter than its diff:
```python
import functools
import math

import jax
import jax.numpy as jnp
from jax import lax
from jax.experimental import pallas as pl
from jax.experimental.pallas import tpu as pltpu
from jax.sharding import PartitionSpec as P

mscale_yarn = 1.0 + 0.1 * math.log(40.0)
masked_score = -1e30
MESH = pl.DeviceIdType.MESH
F32 = jnp.float32
BF16 = jnp.bfloat16
NT = (((1,), (1,)), ((), ()))


def pieces(value):
    out = []
    for _ in range(3):
        piece = value.astype(BF16).astype(F32)
        out.append(piece)
        value = value - piece
    return out


def kernel(
    n, tile, chunk,
    x_hbm, gain_hbm, nope_hbm, ropew_hbm, kup_hbm, vup_hbm, outw_hbm, lat_hbm, crope_hbm, len_hbm,
    out_ref,
    x_v, gain_v, nope_v, ropew_v, kup_v, vup_v, outw_v, lat_v, crope_v, len_s,
    qbuf, score_s, stat_s, pool_s, sb, rb, hvbuf, opart, ob, orb, fin,
    ld_sem,
    kvs, kvr, qs, qr, ps, pr, hs, hr, os, orr, fs, fr, gs, gr,
):
    me = lax.axis_index("ctx")
    chips = n // 2
    chip, c = me // 2, me % 2
    heads, nope_w, lat_w = kup_v.shape
    value_w = vup_hbm.shape[2]
    rows = x_v.shape[0]
    requests, keys, _ = lat_hbm.shape
    chip_keys = 2 * keys
    model = out_ref.shape[1]
    half = model // 2
    stretch = rows // requests
    block_rows = heads * stretch
    rope_w = ropew_v.shape[1] // heads
    q_w = qbuf.shape[3]
    hv_w = heads * value_w
    owners = opart.shape[1]
    base = (chips - owners) // 2
    width = opart.shape[3]
    scale = mscale_yarn * mscale_yarn / math.sqrt(nope_w + rope_w)
    scale2 = scale * math.log2(math.e)
    partner = chip * 2 + 1 - c

    def peer(k):
        flipped, bit = 0, 1
        while bit < chips:
            flipped = flipped + ((chip // bit + (k // bit) % 2) % 2) * bit
            bit *= 2
        return flipped

    near_first = sorted(range(1, chips), key=lambda k: (bin(k).count("1"), k))
    far_first = near_first[::-1]

    def remote(src, dst, ssem, rsem, target):
        return pltpu.make_async_remote_copy(
            src_ref=src, dst_ref=dst, send_sem=ssem, recv_sem=rsem,
            device_id={"ctx": target}, device_id_type=MESH,
        )

    loads = []

    def load(src, dst):
        copy = pltpu.make_async_copy(src, dst, ld_sem.at[len(loads)])
        copy.start()
        loads.append(copy)
        return copy

    barrier = pltpu.get_barrier_semaphore()
    load_x = load(x_hbm, x_v)
    load_gain = load(gain_hbm, gain_v)
    load_nope = load(nope_hbm, nope_v)
    load_rope = load(ropew_hbm, ropew_v)
    load_kup = load(kup_hbm, kup_v)
    load_len = load(len_hbm, len_s)
    for k in far_first:
        pl.semaphore_signal(
            barrier, inc=1, device_id={"ctx": peer(k) * 2 + c}, device_id_type=MESH
        )
    pl.semaphore_signal(barrier, inc=1, device_id={"ctx": partner}, device_id_type=MESH)

    load_x.wait()
    load_gain.wait()
    widened = x_v[...].astype(F32)
    normed = (
        widened
        * lax.rsqrt(jnp.mean(widened * widened, axis=-1, keepdims=True) + 1e-06)
        * gain_v[...].astype(F32).reshape(1, -1)
    ).astype(BF16)
    load_nope.wait()
    query_nope = jnp.dot(normed, nope_v[...], preferred_element_type=F32).astype(BF16)
    load_rope.wait()
    query_rope = jnp.dot(normed, ropew_v[...], preferred_element_type=F32)
    load_kup.wait()

    mine = lambda at: pl.ds(pl.multiple_of(at * keys, 128), keys)
    out_rows = outw_hbm.shape[0]
    columns = lambda at: pl.ds(pl.multiple_of(at * half, 128), half)
    load_cache = []
    for b in range(requests):
        load_cache.append([
            load(lat_hbm.at[b], lat_v.at[b, mine(c)]),
            load(crope_hbm.at[b], crope_v.at[b, :, mine(c)]),
        ])
    load_late = [
        load(vup_hbm.at[h], vup_v.at[:, h * value_w : (h + 1) * value_w]) for h in range(heads)
    ]
    w_rows = lambda at: pl.ds(pl.multiple_of(at * out_rows, out_rows), out_rows)
    load_late.append(load(outw_hbm.at[:, columns(c)], outw_v.at[w_rows(c), :half]))
    if outw_v.shape[1] > half:
        outw_v[:, half:] = jnp.zeros((outw_v.shape[0], outw_v.shape[1] - half), BF16)

    latents = [
        jnp.dot(
            query_nope[:, h * nope_w : (h + 1) * nope_w], kup_v[h], preferred_element_type=F32
        )
        for h in range(heads)
    ]
    for b in range(requests):
        part = slice(b * stretch, (b + 1) * stretch)
        qbuf[b, chip, :, :lat_w] = jnp.concatenate([t[part] for t in latents], axis=0).astype(BF16)
    qbuf[0, chip, :, lat_w:] = jnp.concatenate(
        [
            jnp.concatenate(
                [
                    query_rope[b * stretch : (b + 1) * stretch, h * rope_w : (h + 1) * rope_w]
                    for b in range(requests)
                ],
                axis=1,
            )
            for h in range(heads)
        ],
        axis=0,
    ).astype(BF16)
    pl.semaphore_wait(barrier, chips)

    pending = []

    def send(copy):
        copy.start()
        pending.append(copy)

    def query_copy(b, source, k, target):
        ref = qbuf.at[b, source] if b == 0 else qbuf.at[b, source, :, :lat_w]
        return remote(ref, ref, qs.at[b, k], qr.at[b, k], target)

    def kv_copies(b, side):
        return [
            remote(lat_hbm.at[b], lat_v.at[b, mine(side)], kvs.at[b, 0], kvr.at[b, 0], partner),
            remote(
                crope_hbm.at[b], crope_v.at[b, :, mine(side)], kvs.at[b, 1], kvr.at[b, 1], partner
            ),
        ]

    def w_copy(side):
        return remote(
            outw_hbm.at[:, columns(1 - c)], outw_v.at[w_rows(side), :half],
            kvs.at[requests, 0], kvr.at[requests, 0], partner,
        )

    for b in range(requests):
        for k in far_first:
            send(query_copy(b, chip, k, peer(k) * 2 + c))
    for b in range(requests):
        for copy in kv_copies(b, c):
            send(copy)
    send(w_copy(c))

    load_len.wait()
    first_key = chip * chip_keys
    per_request = chips * block_rows
    tiles = per_request // tile
    tile_chips = tile // block_rows
    lane = lax.broadcasted_iota(jnp.int32, (tile, 128), 1)

    def attend(b, d0):
        query = qbuf[b, pl.ds(d0, tile_chips), :, :lat_w].reshape(tile, lat_w)
        rope_at = lat_w + b * rope_w
        rope = qbuf[0, pl.ds(d0, tile_chips), :, rope_at : rope_at + rope_w].reshape(tile, rope_w)
        row = lax.broadcasted_iota(jnp.int32, (tile, 1), 0) % stretch
        limit = len_s[b] + row - first_key
        peak = None
        for at in range(0, chip_keys, chunk):
            span = slice(at, at + chunk)
            raw = lax.dot_general(query, lat_v[b, span], NT, preferred_element_type=F32)
            raw = raw + jnp.dot(rope, crope_v[b, :, span], preferred_element_type=F32)
            where_key = lax.broadcasted_iota(jnp.int32, (tile, chunk), 1) + at
            raw = jnp.where(where_key <= limit, raw, masked_score)
            score_s[:, span] = raw
            high = jnp.max(raw, axis=1, keepdims=True)
            peak = high if peak is None else jnp.maximum(peak, high)
        total, pooled = None, None
        for at in range(0, chip_keys, chunk):
            span = slice(at, at + chunk)
            weights = jnp.exp2((score_s[:, span] - peak) * scale2)
            part = jnp.sum(weights, axis=1, keepdims=True)
            pool = jnp.dot(weights.astype(BF16), lat_v[b, span], preferred_element_type=F32)
            total = part if total is None else total + part
            pooled = pool if pooled is None else pooled + pool
        peak = jnp.broadcast_to(peak, (tile, 128))
        total = jnp.broadcast_to(total, (tile, 128))
        stat = jnp.zeros((tile, 128), F32)
        for i, piece in enumerate(pieces(peak) + pieces(total)):
            stat = jnp.where(lane == i, piece, stat)
        to = pl.ds(d0, tile_chips)
        sb[b, to, :, :lat_w] = pooled.astype(BF16).reshape(tile_chips, block_rows, lat_w)
        sb[b, to, :, lat_w:] = stat.astype(BF16).reshape(tile_chips, block_rows, 128)
        pool_s[b, to] = pooled.reshape(tile_chips, block_rows, lat_w)
        stat_s[b, to] = jnp.where(lane < 64, peak, total).reshape(tile_chips, block_rows, 128)

    def pool_copy(b, k, slot):
        return remote(
            sb.at[b, peer(k)], rb.at[b, slot], ps.at[b, k], pr.at[b, k], peer(k) * 2 + c
        )

    for b in range(requests):
        for copy in load_cache[b]:
            copy.wait()
        for k in near_first:
            query_copy(b, peer(k), k, peer(k) * 2 + c).wait_recv()
        for copy in kv_copies(b, 1 - c):
            copy.wait_recv()
        if tiles == 1:
            attend(b, 0)
        else:
            def step(t, carry, b=b):
                attend(b, t * tile_chips)
                return carry
            lax.fori_loop(0, tiles, step, 0)
        for k in far_first:
            send(pool_copy(b, k, chip))

    def hv_copy(b, side):
        return remote(hvbuf.at[b, side], hvbuf.at[b, side], hs.at[b], hr.at[b], partner)

    def combine(b):
        own = stat_s[b, chip]
        parts = [(own[:, 0:1], own[:, 64:65], pool_s[b, chip])]
        for k in near_first:
            pool_copy(b, k, peer(k)).wait_recv()
        for k in near_first:
            stat = rb[b, peer(k), :, lat_w:].astype(F32)
            peak = stat[:, 0:1] + stat[:, 1:2] + stat[:, 2:3]
            total = stat[:, 3:4] + stat[:, 4:5] + stat[:, 5:6]
            parts.append((peak, total, rb[b, peer(k), :, :lat_w].astype(F32)))
        top = functools.reduce(jnp.maximum, [peak for peak, _, _ in parts])
        sums, pooled = 0.0, 0.0
        for peak, total, pool in parts:
            factor = jnp.exp2((peak - top) * scale2)
            sums = sums + factor * total
            pooled = pooled + factor * pool
        attended = (pooled / sums).astype(BF16)
        values = jnp.dot(attended, vup_v[...], preferred_element_type=F32)
        hvbuf[b, c] = jnp.concatenate(
            [
                values[h * stretch : (h + 1) * stretch, h * value_w : (h + 1) * value_w]
                for h in range(heads)
            ],
            axis=1,
        ).astype(BF16)
        send(hv_copy(b, c))

    upper = chip // (chips // 2)

    def far_owner(i):
        return (owners - 1 - i) * (1 - upper) + i * upper

    def out_copy(b, o):
        return remote(
            ob.at[b, o], orb.at[b, chip], os.at[b, o], orr.at[b, chip], (base + o) * 2 + c
        )

    def project(b):
        hv_copy(b, 1 - c).wait_recv()
        head_values = jnp.concatenate([hvbuf[b, 0], hvbuf[b, 1]], axis=1)
        for i in range(owners):
            o = far_owner(i)
            at = pl.ds(pl.multiple_of(o * width, 128), width)
            piece = jnp.dot(head_values, outw_v[:, at], preferred_element_type=F32)
            opart[b, o] = piece
            ob[b, o] = piece.astype(BF16)

            @pl.when(chip != base + o)
            def _():
                out_copy(b, o).start()

    is_owner = jnp.logical_and(chip >= base, chip < base + owners)

    def fin_copy(b, o, k):
        return remote(
            fin.at[b, c, o], fin.at[b, c, o], fs.at[b, k], fr.at[b, o], peer(k) * 2 + c
        )

    def relay_copy(b, side, o):
        ref = fin.at[b, side, o]
        return remote(ref, ref, gs.at[b, o], gr.at[b, o], partner)

    def reduce_out(b):
        @pl.when(is_owner)
        def _():
            o = chip - base
            summed = opart[b, o]
            for k in near_first:
                remote(
                    ob.at[b, 0], orb.at[b, peer(k)], os.at[b, 0], orr.at[b, peer(k)],
                    peer(k) * 2 + c,
                ).wait_recv()
            for k in near_first:
                summed = summed + orb[b, peer(k)].astype(F32)
            fin[b, c, o] = summed.astype(BF16)
            for k in far_first:
                fin_copy(b, o, k).start()

    def spread(b):
        for i in reversed(range(owners)):
            o = far_owner(i)

            @pl.when(chip != base + o)
            def _():
                fin_copy(b, o, 1).wait_recv()

            send(relay_copy(b, c, o))

    for copy in load_late:
        copy.wait()
    for b in range(requests):
        combine(b)
        if b == 0:
            w_copy(1 - c).wait_recv()
        project(b)
    for b in range(requests):
        reduce_out(b)
    for b in range(requests):
        spread(b)
    for b in range(requests):
        for i in reversed(range(owners)):
            relay_copy(b, 1 - c, far_owner(i)).wait_recv()

    for side in range(2):
        for o in range(owners):
            used = max(0, min(width, half - o * width))
            if used:
                at = side * half + o * width
                out_ref[:, at : at + used] = jnp.concatenate(
                    [fin[b, side, o, :, :used].astype(F32) for b in range(requests)], axis=0
                ).astype(BF16)
    for copy in pending:
        copy.wait_send()
    for b in range(requests):
        for o in range(owners):
            @pl.when(chip != base + o)
            def _():
                out_copy(b, o).wait_send()

        @pl.when(is_owner)
        def _():
            for k in far_first:
                fin_copy(b, chip - base, k).wait_send()


def local(
    n, query_input, query_gain, nope_weight, rope_weight, key_up, value_up, out_weight,
    cache_latent, cache_rope, cached_length,
):
    heads, _, lat_w = key_up.shape
    value_w = value_up.shape[2]
    rows = query_input.shape[0]
    requests, keys, _ = cache_latent.shape
    rope_w = rope_weight.shape[1] // heads
    stretch = rows // requests
    block_rows = heads * stretch
    model = out_weight.shape[1]
    half = model // 2
    chips = n // 2
    owners = max(1, chips // 2)
    tile = min(128, chips * block_rows)
    chunk = min(1024, 2 * keys)
    width = -(-half // (128 * owners)) * 128
    vmem = pltpu.VMEM
    dma = lambda *count: pltpu.SemaphoreType.DMA(count)
    any_spec = pl.BlockSpec(memory_space=pl.ANY)
    per_block = (requests, chips, block_rows)
    pair = lambda count: [dma(requests, count)] * 2
    return pl.pallas_call(
        functools.partial(kernel, n, tile, chunk),
        out_shape=jax.ShapeDtypeStruct((rows, model), BF16),
        in_specs=[any_spec] * 10,
        out_specs=pl.BlockSpec(memory_space=pltpu.VMEM),
        scratch_shapes=[
            vmem(query_input.shape, BF16), vmem(query_gain.shape, BF16),
            vmem(nope_weight.shape, BF16), vmem(rope_weight.shape, BF16),
            vmem(key_up.shape, BF16), vmem((lat_w, heads * value_w), BF16),
            vmem((2 * out_weight.shape[0], owners * width), BF16),
            vmem((requests, 2 * keys, lat_w), BF16),
            vmem((requests, rope_w, 2 * keys), BF16),
            pltpu.SMEM(cached_length.shape, jnp.int32),
            vmem((*per_block, lat_w + requests * rope_w), BF16),
            vmem((tile, 2 * keys), F32),
            vmem((*per_block, 128), F32), vmem((*per_block, lat_w), F32),
            vmem((*per_block, lat_w + 128), BF16), vmem((*per_block, lat_w + 128), BF16),
            vmem((requests, 2, stretch, heads * value_w), BF16),
            vmem((requests, owners, stretch, width), F32),
            vmem((requests, owners, stretch, width), BF16),
            vmem((requests, chips, stretch, width), BF16),
            vmem((requests, 2, owners, stretch, width), BF16),
            dma(6 + 2 * requests + heads + 1),
            dma(requests + 1, 2), dma(requests + 1, 2),
            *pair(chips), *pair(chips), dma(requests), dma(requests),
            dma(requests, owners), dma(requests, chips),
            dma(requests, chips), dma(requests, owners), *pair(owners),
        ],
        compiler_params=pltpu.CompilerParams(
            collective_id=0, has_side_effects=True, vmem_limit_bytes=63 * 1024 * 1024
        ),
    )(
        query_input, query_gain, nope_weight, rope_weight, key_up,
        value_up, out_weight, cache_latent, cache_rope, cached_length,
    )


def solution(mesh):
    placed = (
        P("groups", None),
        P(),
        P(None, "ctx"),
        P(None, "ctx"),
        P("ctx", None, None),
        P("ctx", None, None),
        P("ctx", None),
        P("groups", "ctx", None),
        P("groups", None, "ctx"),
        P("groups"),
    )
    return jax.shard_map(
        functools.partial(local, mesh.shape["ctx"]), mesh=mesh, in_specs=placed,
        out_specs=P("groups", None), check_vma=False,
    )
```

time: 48.6 us -> 37.3 us (0.77)
  Pallas kernels: 46.8 us -> 35.5 us
    pallas_call x1, Pallas kernels: 46.8 us -> 35.5 us  [local(): pl.pallas_call(functools.partial(kernel, n, tile, chunk), out_shape=jax.S...]
where the time goes in v1:
time: 37.3 us; the launch traced here: 37.1 us
  Pallas kernels  35.5 us (95%)
  local copies, waits for them, and re-layouts  1.64 us (4%)
    pallas_call x1, Pallas kernels, local(): pl.pallas_call(functools.partial(kernel, n, tile, chunk), out_shape=jax.S...  35.5 us
    unnamed x1, local copies, waits for them, and re-layouts  1.64 us

profile of v1, /device:TPU:0, one launch (start us, length us, event | category | flops | bytes accessed | tf_op | source)
XLA Modules:
  0.0 37.1 jit_solution(3041399361925604512)
XLA Ops:
  0.0 35.5 %shard_map.100 = bf16[16,7168]{1,0:T(8,128)(2,1)} custom-call(bf16[16,1536]{1,0:T(8,128)(2,1)} %x_hbm.1, bf16[1536]{0:T(1024)(128)(2,1)} %gain_hbm.1, bf16[1536,256]{1,0:T(8,128)(2,1)} %nope_hbm.1, bf16[1536,128]{1,0:T(8,128)(2,1)} %ropew_hbm.1, bf16[2,128,512]{2,1,0:T(8,128)(2,1)} %kup_hbm.1, bf16[2,512,128]{2,1,0:T(8,128)(2,1)} %vup_hbm.1, ...), custom_call_target="tpu_custom_call" | custom-call | tf_op jit(solution)/shard_map/pallas_call | solution.py:398
  35.5 1.6 %copy.12 = bf16[16,7168]{1,0:T(8,128)(2,1)} copy(bf16[16,7168]{1,0:T(8,128)(2,1)} %shard_map.100) | data formatting | bytes 458752

commit v2 on v1

--- a/solution.py
+++ b/solution.py
@@ -31,8 +31,7 @@
     out_ref,
     x_v, gain_v, nope_v, ropew_v, kup_v, vup_v, outw_v, lat_v, crope_v, len_s,
     qbuf, score_s, stat_s, pool_s, sb, rb, hvbuf, opart, ob, orb, fin,
-    ld_sem,
-    kvs, kvr, qs, qr, ps, pr, hs, hr, os, orr, fs, fr, gs, gr,
+    ld_sem, kvs, kvr, qs, qr, pr, hr, os, orr, fs, fr, gs, gr,
 ):
     me = lax.axis_index("ctx")
     chips = n // 2
@@ -72,21 +71,18 @@
             device_id={"ctx": target}, device_id_type=MESH,
         )
 
-    loads = []
-
-    def load(src, dst):
-        copy = pltpu.make_async_copy(src, dst, ld_sem.at[len(loads)])
+    def load(src, dst, slot):
+        copy = pltpu.make_async_copy(src, dst, ld_sem.at[slot])
         copy.start()
-        loads.append(copy)
         return copy
 
     barrier = pltpu.get_barrier_semaphore()
-    load_x = load(x_hbm, x_v)
-    load_gain = load(gain_hbm, gain_v)
-    load_nope = load(nope_hbm, nope_v)
-    load_rope = load(ropew_hbm, ropew_v)
-    load_kup = load(kup_hbm, kup_v)
-    load_len = load(len_hbm, len_s)
+    load_x = load(x_hbm, x_v, 0)
+    load_gain = load(gain_hbm, gain_v, 1)
+    load_nope = load(nope_hbm, nope_v, 2)
+    load_rope = load(ropew_hbm, ropew_v, 3)
+    load_kup = load(kup_hbm, kup_v, 4)
+    load_len = load(len_hbm, len_s, 5)
     for k in far_first:
         pl.semaphore_signal(
             barrier, inc=1, device_id={"ctx": peer(k) * 2 + c}, device_id_type=MESH
@@ -106,21 +102,21 @@
     load_rope.wait()
     query_rope = jnp.dot(normed, ropew_v[...], preferred_element_type=F32)
     load_kup.wait()
+    load_len.wait()
 
     mine = lambda at: pl.ds(pl.multiple_of(at * keys, 128), keys)
     out_rows = outw_hbm.shape[0]
     columns = lambda at: pl.ds(pl.multiple_of(at * half, 128), half)
-    load_cache = []
-    for b in range(requests):
-        load_cache.append([
-            load(lat_hbm.at[b], lat_v.at[b, mine(c)]),
-            load(crope_hbm.at[b], crope_v.at[b, :, mine(c)]),
-        ])
+    w_rows = lambda at: pl.ds(pl.multiple_of(at * out_rows, out_rows), out_rows)
+    load_crope = load(crope_hbm, crope_v.at[:, :, mine(c)], 0)
+    load_lat = [load(lat_hbm.at[b], lat_v.at[b, mine(c)], 1 + b) for b in range(requests)]
     load_late = [
-        load(vup_hbm.at[h], vup_v.at[:, h * value_w : (h + 1) * value_w]) for h in range(heads)
+        load(vup_hbm.at[h], vup_v.at[:, h * value_w : (h + 1) * value_w], 1 + requests + h)
+        for h in range(heads)
     ]
-    w_rows = lambda at: pl.ds(pl.multiple_of(at * out_rows, out_rows), out_rows)
-    load_late.append(load(outw_hbm.at[:, columns(c)], outw_v.at[w_rows(c), :half]))
+    load_late.append(
+        load(outw_hbm.at[:, columns(c)], outw_v.at[w_rows(c), :half], 1 + requests + heads)
+    )
     if outw_v.shape[1] > half:
         outw_v[:, half:] = jnp.zeros((outw_v.shape[0], outw_v.shape[1] - half), BF16)
 
@@ -148,39 +144,43 @@
     ).astype(BF16)
     pl.semaphore_wait(barrier, chips)
 
-    pending = []
-
-    def send(copy):
-        copy.start()
-        pending.append(copy)
-
-    def query_copy(b, source, k, target):
-        ref = qbuf.at[b, source] if b == 0 else qbuf.at[b, source, :, :lat_w]
-        return remote(ref, ref, qs.at[b, k], qr.at[b, k], target)
-
-    def kv_copies(b, side):
-        return [
-            remote(lat_hbm.at[b], lat_v.at[b, mine(side)], kvs.at[b, 0], kvr.at[b, 0], partner),
-            remote(
-                crope_hbm.at[b], crope_v.at[b, :, mine(side)], kvs.at[b, 1], kvr.at[b, 1], partner
-            ),
-        ]
+    others = pl.ds(0, chips - 1)
+
+    def sent(ref, sem):
+        remote(ref, ref, sem, sem, partner).wait_send()
+
+    def received(ref, sem):
+        remote(ref, ref, sem, sem, partner).wait_recv()
+
+    def queries(b, at):
+        return qbuf.at[b, at] if b == 0 else qbuf.at[b, at, :, :lat_w]
+
+    def lat_copy(b, side):
+        return remote(lat_hbm.at[b], lat_v.at[b, mine(side)], kvs.at[b], kvr.at[b], partner)
+
+    def crope_copy(side):
+        return remote(
+            crope_hbm, crope_v.at[:, :, mine(side)], kvs.at[requests], kvr.at[requests], partner
+        )
 
     def w_copy(side):
         return remote(
             outw_hbm.at[:, columns(1 - c)], outw_v.at[w_rows(side), :half],
-            kvs.at[requests, 0], kvr.at[requests, 0], partner,
-        )
-
-    for b in range(requests):
-        for k in far_first:
-            send(query_copy(b, chip, k, peer(k) * 2 + c))
-    for b in range(requests):
-        for copy in kv_copies(b, c):
-            send(copy)
-    send(w_copy(c))
-
-    load_len.wait()
+            kvs.at[requests + 1], kvr.at[requests + 1], partner,
+        )
+
+    def send_queries(b, ks):
+        for k in ks:
+            ref = queries(b, chip)
+            remote(ref, ref, qs.at[b], qr.at[b], peer(k) * 2 + c).start()
+
+    send_queries(0, far_first)
+    crope_copy(c).start()
+    for b in range(requests):
+        lat_copy(b, c).start()
+    received(queries(0, others), qr.at[0])
+    for b in range(1, requests):
+        send_queries(b, far_first)
     first_key = chip * chip_keys
     per_request = chips * block_rows
     tiles = per_request // tile
@@ -222,18 +222,15 @@
         pool_s[b, to] = pooled.reshape(tile_chips, block_rows, lat_w)
         stat_s[b, to] = jnp.where(lane < 64, peak, total).reshape(tile_chips, block_rows, 128)
 
-    def pool_copy(b, k, slot):
-        return remote(
-            sb.at[b, peer(k)], rb.at[b, slot], ps.at[b, k], pr.at[b, k], peer(k) * 2 + c
-        )
-
-    for b in range(requests):
-        for copy in load_cache[b]:
-            copy.wait()
-        for k in near_first:
-            query_copy(b, peer(k), k, peer(k) * 2 + c).wait_recv()
-        for copy in kv_copies(b, 1 - c):
-            copy.wait_recv()
+    for b in range(requests):
+        load_lat[b].wait()
+        if b == 0:
+            load_crope.wait()
+        if b:
+            received(queries(b, others), qr.at[b])
+        if b == 0:
+            crope_copy(1 - c).wait_recv()
+        lat_copy(b, 1 - c).wait_recv()
         if tiles == 1:
             attend(b, 0)
         else:
@@ -241,17 +238,21 @@
                 attend(b, t * tile_chips)
                 return carry
             lax.fori_loop(0, tiles, step, 0)
+        sent(queries(b, others), qs.at[b])
         for k in far_first:
-            send(pool_copy(b, k, chip))
+            remote(
+                sb.at[b, peer(k)], rb.at[b, chip], qs.at[b], pr.at[b], peer(k) * 2 + c
+            ).start()
+        if b == 0:
+            w_copy(c).start()
 
     def hv_copy(b, side):
-        return remote(hvbuf.at[b, side], hvbuf.at[b, side], hs.at[b], hr.at[b], partner)
+        return remote(hvbuf.at[b, side], hvbuf.at[b, side], qs.at[b], hr.at[b], partner)
 
     def combine(b):
         own = stat_s[b, chip]
         parts = [(own[:, 0:1], own[:, 64:65], pool_s[b, chip])]
-        for k in near_first:
-            pool_copy(b, k, peer(k)).wait_recv()
+        received(rb.at[b, others], pr.at[b])
         for k in near_first:
             stat = rb[b, peer(k), :, lat_w:].astype(F32)
             peak = stat[:, 0:1] + stat[:, 1:2] + stat[:, 2:3]
@@ -272,7 +273,8 @@
             ],
             axis=1,
         ).astype(BF16)
-        send(hv_copy(b, c))
+        sent(sb.at[b, others], qs.at[b])
+        hv_copy(b, c).start()
 
     upper = chip // (chips // 2)
 
@@ -281,7 +283,7 @@
 
     def out_copy(b, o):
         return remote(
-            ob.at[b, o], orb.at[b, chip], os.at[b, o], orr.at[b, chip], (base + o) * 2 + c
+            ob.at[b, o], orb.at[b, chip], os.at[b], orr.at[b], (base + o) * 2 + c
         )
 
     def project(b):
@@ -301,39 +303,47 @@
     is_owner = jnp.logical_and(chip >= base, chip < base + owners)
 
     def fin_copy(b, o, k):
-        return remote(
-            fin.at[b, c, o], fin.at[b, c, o], fs.at[b, k], fr.at[b, o], peer(k) * 2 + c
-        )
-
-    def relay_copy(b, side, o):
-        ref = fin.at[b, side, o]
-        return remote(ref, ref, gs.at[b, o], gr.at[b, o], partner)
+        ref = fin.at[b, c, o]
+        return remote(ref, ref, fs.at[b], fr.at[b], peer(k) * 2 + c)
+
+    def relay_copy(b, side):
+        ref = fin.at[b, side]
+        return remote(ref, ref, gs.at[b], gr.at[b], partner)
 
     def reduce_out(b):
         @pl.when(is_owner)
         def _():
             o = chip - base
+            received(orb.at[b, others], orr.at[b])
             summed = opart[b, o]
-            for k in near_first:
-                remote(
-                    ob.at[b, 0], orb.at[b, peer(k)], os.at[b, 0], orr.at[b, peer(k)],
-                    peer(k) * 2 + c,
-                ).wait_recv()
             for k in near_first:
                 summed = summed + orb[b, peer(k)].astype(F32)
             fin[b, c, o] = summed.astype(BF16)
             for k in far_first:
                 fin_copy(b, o, k).start()
 
-    def spread(b):
-        for i in reversed(range(owners)):
-            o = far_owner(i)
-
-            @pl.when(chip != base + o)
+    def by_role(wait):
+        if owners > 1:
+            @pl.when(is_owner)
             def _():
-                fin_copy(b, o, 1).wait_recv()
-
-            send(relay_copy(b, c, o))
+                wait(pl.ds(0, owners - 1))
+
+        @pl.when(jnp.logical_not(is_owner))
+        def _():
+            wait(pl.ds(0, owners))
+
+    def place(side):
+        for core in range(2):
+            @pl.when(side == core)
+            def _():
+                for o in range(owners):
+                    used = min(width, half - o * width)
+                    if used > 0:
+                        at = core * half + o * width
+                        out_ref[:, at : at + used] = jnp.concatenate(
+                            [fin[b, core, o, :, :used].astype(F32) for b in range(requests)],
+                            axis=0,
+                        ).astype(BF16)
 
     for copy in load_late:
         copy.wait()
@@ -344,32 +354,27 @@
         project(b)
     for b in range(requests):
         reduce_out(b)
-    for b in range(requests):
-        spread(b)
-    for b in range(requests):
-        for i in reversed(range(owners)):
-            relay_copy(b, 1 - c, far_owner(i)).wait_recv()
-
-    for side in range(2):
-        for o in range(owners):
-            used = max(0, min(width, half - o * width))
-            if used:
-                at = side * half + o * width
-                out_ref[:, at : at + used] = jnp.concatenate(
-                    [fin[b, side, o, :, :used].astype(F32) for b in range(requests)], axis=0
-                ).astype(BF16)
-    for copy in pending:
-        copy.wait_send()
-    for b in range(requests):
-        for o in range(owners):
-            @pl.when(chip != base + o)
-            def _():
-                out_copy(b, o).wait_send()
-
-        @pl.when(is_owner)
-        def _():
-            for k in far_first:
-                fin_copy(b, chip - base, k).wait_send()
+    crope_copy(c).wait_send()
+    for b in range(requests):
+        lat_copy(b, c).wait_send()
+        sent(hvbuf.at[b, c], qs.at[b])
+        by_role(lambda part: sent(ob.at[b, part], os.at[b]))
+    w_copy(c).wait_send()
+    for b in range(requests):
+        by_role(lambda part: received(fin.at[b, c, part], fr.at[b]))
+        relay_copy(b, c).start()
+    place(c)
+
+    @pl.when(is_owner)
+    def _():
+        for b in range(requests):
+            sent(orb.at[b, others], fs.at[b])
+
+    for b in range(requests):
+        relay_copy(b, 1 - c).wait_recv()
+    place(1 - c)
+    for b in range(requests):
+        relay_copy(b, c).wait_send()
 
 
 def local(
@@ -394,7 +399,6 @@
     dma = lambda *count: pltpu.SemaphoreType.DMA(count)
     any_spec = pl.BlockSpec(memory_space=pl.ANY)
     per_block = (requests, chips, block_rows)
-    pair = lambda count: [dma(requests, count)] * 2
     return pl.pallas_call(
         functools.partial(kernel, n, tile, chunk),
         out_shape=jax.ShapeDtypeStruct((rows, model), BF16),
@@ -417,19 +421,19 @@
             vmem((requests, owners, stretch, width), BF16),
             vmem((requests, chips, stretch, width), BF16),
             vmem((requests, 2, owners, stretch, width), BF16),
-            dma(6 + 2 * requests + heads + 1),
-            dma(requests + 1, 2), dma(requests + 1, 2),
-            *pair(chips), *pair(chips), dma(requests), dma(requests),
-            dma(requests, owners), dma(requests, chips),
-            dma(requests, chips), dma(requests, owners), *pair(owners),
+            dma(max(6, 2 + requests + heads)), dma(requests + 2), dma(requests + 2),
+            *[dma(requests)] * 10,
         ],
         compiler_params=pltpu.CompilerParams(
-            collective_id=0, has_side_effects=True, vmem_limit_bytes=63 * 1024 * 1024
+            collective_id=0, has_side_effects=True, vmem_limit_bytes=40 * 1024 * 1024
         ),
-    )(
-        query_input, query_gain, nope_weight, rope_weight, key_up,
-        value_up, out_weight, cache_latent, cache_rope, cached_length,
-    )
+    )(*[
+        pltpu.with_memory_space_constraint(array, pltpu.HBM)
+        for array in (
+            query_input, query_gain, nope_weight, rope_weight, key_up,
+            value_up, out_weight, cache_latent, cache_rope, cached_length,
+        )
+    ])
 
 
 def solution(mesh):

time: 37.3 us -> 34 us (0.912)
  Pallas kernels: 35.5 us -> 33.1 us
  local copies, waits for them, and re-layouts: 1.64 us -> 0.69 us
    pallas_call x1, Pallas kernels: 35.5 us -> 33.1 us  [local(): pl.pallas_call(functools.partial(kernel, n, tile, chunk), out_shape=jax.S...]
    unnamed x1, local copies, waits for them, and re-layouts: 1.64 us -> 0.69 us
where the time goes in v2:
time: 34 us; the launch traced here: 33.8 us
  Pallas kernels  33.1 us (97%)
  local copies, waits for them, and re-layouts  0.69 us (2%)
    pallas_call x1, Pallas kernels, local(): pl.pallas_call(functools.partial(kernel, n, tile, chunk), out_shape=jax.S...  33.1 us
    unnamed x1, local copies, waits for them, and re-layouts  0.69 us

profile of v2, /device:TPU:0, one launch (start us, length us, event | category | flops | bytes accessed | tf_op | source)
XLA Modules:
  0.0 33.8 jit_solution(12756042271151606045)
XLA Ops:
  0.0 33.1 %shard_map.100 = bf16[16,7168]{1,0:T(8,128)(2,1)S(1)} custom-call(bf16[16,1536]{1,0:T(8,128)(2,1)} %x_hbm.1, bf16[1536]{0:T(1024)(128)(2,1)} %gain_hbm.1, bf16[1536,256]{1,0:T(8,128)(2,1)} %nope_hbm.1, bf16[1536,128]{1,0:T(8,128)(2,1)} %ropew_hbm.1, bf16[2,128,512]{2,1,0:T(8,128)(2,1)} %kup_hbm.1, bf16[2,512,128]{2,1,0:T(8,128)(2,1)} %vup_hbm.1, ...), custom_call_target="tpu_custom_call" | custom-call | tf_op jit(solution)/shard_map/pallas_call | solution.py:402
  33.1 0.7 %copy.12 = bf16[16,7168]{1,0:T(8,128)(2,1)} copy(bf16[16,7168]{1,0:T(8,128)(2,1)S(1)} %shard_map.100) | data formatting | bytes 458752

commit v3 on v2

--- a/solution.py
+++ b/solution.py
@@ -16,22 +16,13 @@
 NT = (((1,), (1,)), ((), ()))
 
 
-def pieces(value):
-    out = []
-    for _ in range(3):
-        piece = value.astype(BF16).astype(F32)
-        out.append(piece)
-        value = value - piece
-    return out
-
-
 def kernel(
     n, tile, chunk,
     x_hbm, gain_hbm, nope_hbm, ropew_hbm, kup_hbm, vup_hbm, outw_hbm, lat_hbm, crope_hbm, len_hbm,
     out_ref,
     x_v, gain_v, nope_v, ropew_v, kup_v, vup_v, outw_v, lat_v, crope_v, len_s,
-    qbuf, score_s, stat_s, pool_s, sb, rb, hvbuf, opart, ob, orb, fin,
-    ld_sem, kvs, kvr, qs, qr, pr, hr, os, orr, fs, fr, gs, gr,
+    qbuf, score_s, stat_b, turn_s, pool_s, sb, rb, hvbuf, opart, ob, orb, fin,
+    ld_sem, kvs, kvr, qs, qr, ts, tr, pr, hr, os, orr, fs, fr, gs, gr,
 ):
     me = lax.axis_index("ctx")
     chips = n // 2
@@ -98,12 +89,34 @@
         * gain_v[...].astype(F32).reshape(1, -1)
     ).astype(BF16)
     load_nope.wait()
-    query_nope = jnp.dot(normed, nope_v[...], preferred_element_type=F32).astype(BF16)
     load_rope.wait()
-    query_rope = jnp.dot(normed, ropew_v[...], preferred_element_type=F32)
     load_kup.wait()
     load_len.wait()
-
+    query_nope = jnp.dot(normed, nope_v[...], preferred_element_type=F32).astype(BF16)
+    query_rope = jnp.dot(normed, ropew_v[...], preferred_element_type=F32)
+
+    latents = [
+        jnp.dot(
+            query_nope[:, h * nope_w : (h + 1) * nope_w], kup_v[h], preferred_element_type=F32
+        )
+        for h in range(heads)
+    ]
+    for b in range(requests):
+        part = slice(b * stretch, (b + 1) * stretch)
+        qbuf[b, chip, :, :lat_w] = jnp.concatenate([t[part] for t in latents], axis=0).astype(BF16)
+    qbuf[0, chip, :, lat_w:] = jnp.concatenate(
+        [
+            jnp.concatenate(
+                [
+                    query_rope[b * stretch : (b + 1) * stretch, h * rope_w : (h + 1) * rope_w]
+                    for b in range(requests)
+                ],
+                axis=1,
+            )
+            for h in range(heads)
+        ],
+        axis=0,
+    ).astype(BF16)
     mine = lambda at: pl.ds(pl.multiple_of(at * keys, 128), keys)
     out_rows = outw_hbm.shape[0]
     columns = lambda at: pl.ds(pl.multiple_of(at * half, 128), half)
@@ -120,28 +133,6 @@
     if outw_v.shape[1] > half:
         outw_v[:, half:] = jnp.zeros((outw_v.shape[0], outw_v.shape[1] - half), BF16)
 
-    latents = [
-        jnp.dot(
-            query_nope[:, h * nope_w : (h + 1) * nope_w], kup_v[h], preferred_element_type=F32
-        )
-        for h in range(heads)
-    ]
-    for b in range(requests):
-        part = slice(b * stretch, (b + 1) * stretch)
-        qbuf[b, chip, :, :lat_w] = jnp.concatenate([t[part] for t in latents], axis=0).astype(BF16)
-    qbuf[0, chip, :, lat_w:] = jnp.concatenate(
-        [
-            jnp.concatenate(
-                [
-                    query_rope[b * stretch : (b + 1) * stretch, h * rope_w : (h + 1) * rope_w]
-                    for b in range(requests)
-                ],
-                axis=1,
-            )
-            for h in range(heads)
-        ],
-        axis=0,
-    ).astype(BF16)
     pl.semaphore_wait(barrier, chips)
 
     others = pl.ds(0, chips - 1)
@@ -178,9 +169,19 @@
     crope_copy(c).start()
     for b in range(requests):
         lat_copy(b, c).start()
-    received(queries(0, others), qr.at[0])
+    crope_copy(1 - c).wait_recv()
+
+    @pl.when(c == 1)
+    def _():
+        received(queries(0, others), qr.at[0])
+
     for b in range(1, requests):
         send_queries(b, far_first)
+
+    @pl.when(c != 1)
+    def _():
+        received(queries(0, others), qr.at[0])
+
     first_key = chip * chip_keys
     per_request = chips * block_rows
     tiles = per_request // tile
@@ -195,10 +196,15 @@
         limit = len_s[b] + row - first_key
         peak = None
         for at in range(0, chip_keys, chunk):
+            if at == keys:
+                if tiles == 1:
+                    lat_copy(b, 1 - c).wait_recv()
             span = slice(at, at + chunk)
-            raw = lax.dot_general(query, lat_v[b, span], NT, preferred_element_type=F32)
-            raw = raw + jnp.dot(rope, crope_v[b, :, span], preferred_element_type=F32)
-            where_key = lax.broadcasted_iota(jnp.int32, (tile, chunk), 1) + at
+            begin = (at + c * keys) % chip_keys
+            keyed = pl.ds(pl.multiple_of(begin, chunk), chunk)
+            raw = lax.dot_general(query, lat_v[b, keyed], NT, preferred_element_type=F32)
+            raw = raw + jnp.dot(rope, crope_v[b, :, keyed], preferred_element_type=F32)
+            where_key = lax.broadcasted_iota(jnp.int32, (tile, chunk), 1) + begin
             raw = jnp.where(where_key <= limit, raw, masked_score)
             score_s[:, span] = raw
             high = jnp.max(raw, axis=1, keepdims=True)
@@ -206,21 +212,18 @@
         total, pooled = None, None
         for at in range(0, chip_keys, chunk):
             span = slice(at, at + chunk)
+            begin = (at + c * keys) % chip_keys
+            keyed = pl.ds(pl.multiple_of(begin, chunk), chunk)
             weights = jnp.exp2((score_s[:, span] - peak) * scale2)
             part = jnp.sum(weights, axis=1, keepdims=True)
-            pool = jnp.dot(weights.astype(BF16), lat_v[b, span], preferred_element_type=F32)
+            pool = jnp.dot(weights.astype(BF16), lat_v[b, keyed], preferred_element_type=F32)
             total = part if total is None else total + part
             pooled = pool if pooled is None else pooled + pool
-        peak = jnp.broadcast_to(peak, (tile, 128))
-        total = jnp.broadcast_to(total, (tile, 128))
-        stat = jnp.zeros((tile, 128), F32)
-        for i, piece in enumerate(pieces(peak) + pieces(total)):
-            stat = jnp.where(lane == i, piece, stat)
+        stat = jnp.transpose(jnp.where(lane == 0, peak, total))
+        stat_b[b, chip, :, pl.ds(pl.multiple_of(d0 * block_rows, 128), tile)] = stat[:2]
         to = pl.ds(d0, tile_chips)
-        sb[b, to, :, :lat_w] = pooled.astype(BF16).reshape(tile_chips, block_rows, lat_w)
-        sb[b, to, :, lat_w:] = stat.astype(BF16).reshape(tile_chips, block_rows, 128)
+        sb[b, to] = pooled.astype(BF16).reshape(tile_chips, block_rows, lat_w)
         pool_s[b, to] = pooled.reshape(tile_chips, block_rows, lat_w)
-        stat_s[b, to] = jnp.where(lane < 64, peak, total).reshape(tile_chips, block_rows, 128)
 
     for b in range(requests):
         load_lat[b].wait()
@@ -228,9 +231,8 @@
             load_crope.wait()
         if b:
             received(queries(b, others), qr.at[b])
-        if b == 0:
-            crope_copy(1 - c).wait_recv()
-        lat_copy(b, 1 - c).wait_recv()
+        if tiles > 1:
+            lat_copy(b, 1 - c).wait_recv()
         if tiles == 1:
             attend(b, 0)
         else:
@@ -240,6 +242,9 @@
             lax.fori_loop(0, tiles, step, 0)
         sent(queries(b, others), qs.at[b])
         for k in far_first:
+            ref = stat_b.at[b, chip]
+            remote(ref, ref, ts.at[b], tr.at[b], peer(k) * 2 + c).start()
+        for k in far_first:
             remote(
                 sb.at[b, peer(k)], rb.at[b, chip], qs.at[b], pr.at[b], peer(k) * 2 + c
             ).start()
@@ -250,21 +255,26 @@
         return remote(hvbuf.at[b, side], hvbuf.at[b, side], qs.at[b], hr.at[b], partner)
 
     def combine(b):
-        own = stat_s[b, chip]
-        parts = [(own[:, 0:1], own[:, 64:65], pool_s[b, chip])]
+        received(stat_b.at[b, others], tr.at[b])
+        peaks, totals = stat_b[b, :, 0, :], stat_b[b, :, 1, :]
+        factors = jnp.exp2((peaks - jnp.max(peaks, axis=0, keepdims=True)) * scale2)
+        factors = factors / jnp.sum(factors * totals, axis=0, keepdims=True)
+        factors = jnp.concatenate([factors, jnp.zeros((128 - chips, per_request), F32)], axis=0)
+        for at in range(0, per_request, 128):
+            turn_s[at : at + 128] = jnp.transpose(factors[:, at : at + 128])
+        mine = turn_s[pl.ds(pl.multiple_of(chip * block_rows, block_rows), block_rows)]
+        lane = lax.broadcasted_iota(jnp.int32, (block_rows, 128), 1)
+
+        def factor(at):
+            return jnp.sum(jnp.where(lane == at, mine, 0.0), axis=1, keepdims=True)
+
+        weight = [factor(peer(k)) for k in near_first]
+        attended = factor(chip) * pool_s[b, chip]
         received(rb.at[b, others], pr.at[b])
-        for k in near_first:
-            stat = rb[b, peer(k), :, lat_w:].astype(F32)
-            peak = stat[:, 0:1] + stat[:, 1:2] + stat[:, 2:3]
-            total = stat[:, 3:4] + stat[:, 4:5] + stat[:, 5:6]
-            parts.append((peak, total, rb[b, peer(k), :, :lat_w].astype(F32)))
-        top = functools.reduce(jnp.maximum, [peak for peak, _, _ in parts])
-        sums, pooled = 0.0, 0.0
-        for peak, total, pool in parts:
-            factor = jnp.exp2((peak - top) * scale2)
-            sums = sums + factor * total
-            pooled = pooled + factor * pool
-        attended = (pooled / sums).astype(BF16)
+        for i, k in enumerate(near_first):
+            attended = attended + weight[i] * rb[b, peer(k)].astype(F32)
+        attended = attended.astype(BF16)
+        sent(stat_b.at[b, others], ts.at[b])
         values = jnp.dot(attended, vup_v[...], preferred_element_type=F32)
         hvbuf[b, c] = jnp.concatenate(
             [
@@ -393,7 +403,7 @@
     chips = n // 2
     owners = max(1, chips // 2)
     tile = min(128, chips * block_rows)
-    chunk = min(1024, 2 * keys)
+    chunk = min(512, 2 * keys)
     width = -(-half // (128 * owners)) * 128
     vmem = pltpu.VMEM
     dma = lambda *count: pltpu.SemaphoreType.DMA(count)
@@ -414,15 +424,16 @@
             pltpu.SMEM(cached_length.shape, jnp.int32),
             vmem((*per_block, lat_w + requests * rope_w), BF16),
             vmem((tile, 2 * keys), F32),
-            vmem((*per_block, 128), F32), vmem((*per_block, lat_w), F32),
-            vmem((*per_block, lat_w + 128), BF16), vmem((*per_block, lat_w + 128), BF16),
+            vmem((requests, chips, 2, chips * block_rows), F32),
+            vmem((chips * block_rows, 128), F32), vmem((*per_block, lat_w), F32),
+            vmem((*per_block, lat_w), BF16), vmem((*per_block, lat_w), BF16),
             vmem((requests, 2, stretch, heads * value_w), BF16),
             vmem((requests, owners, stretch, width), F32),
             vmem((requests, owners, stretch, width), BF16),
             vmem((requests, chips, stretch, width), BF16),
             vmem((requests, 2, owners, stretch, width), BF16),
             dma(max(6, 2 + requests + heads)), dma(requests + 2), dma(requests + 2),
-            *[dma(requests)] * 10,
+            *[dma(requests)] * 12,
         ],
         compiler_params=pltpu.CompilerParams(
             collective_id=0, has_side_effects=True, vmem_limit_bytes=40 * 1024 * 1024

time: 34 us -> 32.8 us (0.965)
  Pallas kernels: 33.1 us -> 32 us
    pallas_call x1, Pallas kernels: 33.1 us -> 32 us  [local(): pl.pallas_call(functools.partial(kernel, n, tile, chunk), out_shape=jax.S...]
where the time goes in v3:
time: 32.8 us; the launch traced here: 32.7 us
  Pallas kernels  32 us (98%)
  local copies, waits for them, and re-layouts  0.69 us (2%)
    pallas_call x1, Pallas kernels, local(): pl.pallas_call(functools.partial(kernel, n, tile, chunk), out_shape=jax.S...  32 us
    unnamed x1, local copies, waits for them, and re-layouts  0.69 us

profile of v3, /device:TPU:0, one launch (start us, length us, event | category | flops | bytes accessed | tf_op | source)
XLA Modules:
  0.0 32.7 jit_solution(18362276763191006861)
XLA Ops:
  0.0 32.0 %shard_map.100 = bf16[16,7168]{1,0:T(8,128)(2,1)S(1)} custom-call(bf16[16,1536]{1,0:T(8,128)(2,1)} %x_hbm.1, bf16[1536]{0:T(1024)(128)(2,1)} %gain_hbm.1, bf16[1536,256]{1,0:T(8,128)(2,1)} %nope_hbm.1, bf16[1536,128]{1,0:T(8,128)(2,1)} %ropew_hbm.1, bf16[2,128,512]{2,1,0:T(8,128)(2,1)} %kup_hbm.1, bf16[2,512,128]{2,1,0:T(8,128)(2,1)} %vup_hbm.1, ...), custom_call_target="tpu_custom_call" | custom-call | tf_op jit(solution)/shard_map/pallas_call | solution.py:412
  32.0 0.7 %copy.12 = bf16[16,7168]{1,0:T(8,128)(2,1)} copy(bf16[16,7168]{1,0:T(8,128)(2,1)S(1)} %shard_map.100) | data formatting | bytes 458752

commit v4 on v3

v4 whole, which is shorter than its diff:
```python
import functools
import math

import jax
import jax.numpy as jnp
from jax import lax
from jax.experimental import pallas as pl
from jax.experimental.pallas import tpu as pltpu
from jax.sharding import PartitionSpec as P

mscale_yarn = 1.0 + 0.1 * math.log(40.0)
masked_score = -1e30
MESH = pl.DeviceIdType.MESH
F32 = jnp.float32
BF16 = jnp.bfloat16
NT = (((1,), (1,)), ((), ()))


def kernel(
    n, tile, chunk,
    x_hbm, gain_hbm, nope_hbm, ropew_hbm, kup_hbm, vup_hbm, outw_hbm, lat_hbm, crope_hbm, len_hbm,
    out_ref,
    x_v, gain_v, nope_v, ropew_v, kup_v, vup_v, outw_v, lat_v, crope_v, len_s,
    qown, qbuf, score_s, stat_b, turn_s, pool_s, sb, rb, opart, ob, orb, fin,
    ld_sem, kvs, kvr, qs, qr, ts, tr, pr, os, orr, fs, fr, gs, gr,
):
    me = lax.axis_index("ctx")
    chips = n // 2
    chip, c = me // 2, me % 2
    heads, nope_w, lat_w = kup_v.shape
    value_w = vup_hbm.shape[2]
    rows = x_v.shape[0]
    requests, keys, _ = lat_hbm.shape
    chip_keys = 2 * keys
    model = out_ref.shape[1]
    stretch = rows // requests
    block_rows = heads * stretch
    rope_w = ropew_v.shape[1] // heads
    q_w = qbuf.shape[3]
    owners = opart.shape[1]
    base = (chips - owners) // 2
    width = opart.shape[3]
    scale = mscale_yarn * mscale_yarn / math.sqrt(nope_w + rope_w)
    scale2 = scale * math.log2(math.e)
    partner = chip * 2 + 1 - c

    def peer(k):
        flipped, bit = 0, 1
        while bit < chips:
            flipped = flipped + ((chip // bit + (k // bit) % 2) % 2) * bit
            bit *= 2
        return flipped

    near_first = sorted(range(1, chips), key=lambda k: (bin(k).count("1"), k))
    far_first = near_first[::-1]

    def remote(src, dst, ssem, rsem, target):
        return pltpu.make_async_remote_copy(
            src_ref=src, dst_ref=dst, send_sem=ssem, recv_sem=rsem,
            device_id={"ctx": target}, device_id_type=MESH,
        )

    def load(src, dst, slot):
        copy = pltpu.make_async_copy(src, dst, ld_sem.at[slot])
        copy.start()
        return copy

    barrier = pltpu.get_barrier_semaphore()
    load_x = load(x_hbm, x_v, 0)
    load_gain = load(gain_hbm, gain_v, 1)
    load_nope = load(nope_hbm, nope_v, 2)
    load_rope = load(ropew_hbm, ropew_v, 3)
    load_kup = load(kup_hbm, kup_v, 4)
    load_len = load(len_hbm, len_s, 5)
    for k in far_first:
        pl.semaphore_signal(
            barrier, inc=1, device_id={"ctx": peer(k) * 2 + 1 - c}, device_id_type=MESH
        )
    pl.semaphore_signal(barrier, inc=1, device_id={"ctx": partner}, device_id_type=MESH)

    load_x.wait()
    load_gain.wait()
    widened = x_v[...].astype(F32)
    normed = (
        widened
        * lax.rsqrt(jnp.mean(widened * widened, axis=-1, keepdims=True) + 1e-06)
        * gain_v[...].astype(F32).reshape(1, -1)
    ).astype(BF16)
    load_nope.wait()
    load_rope.wait()
    load_kup.wait()
    load_len.wait()
    query_nope = jnp.dot(normed, nope_v[...], preferred_element_type=F32).astype(BF16)
    query_rope = jnp.dot(normed, ropew_v[...], preferred_element_type=F32)

    latents = [
        jnp.dot(
            query_nope[:, h * nope_w : (h + 1) * nope_w], kup_v[h], preferred_element_type=F32
        )
        for h in range(heads)
    ]
    for b in range(requests):
        part = slice(b * stretch, (b + 1) * stretch)
        qown[b, :, :lat_w] = jnp.concatenate([t[part] for t in latents], axis=0).astype(BF16)
    qown[0, :, lat_w:] = jnp.concatenate(
        [
            jnp.concatenate(
                [
                    query_rope[b * stretch : (b + 1) * stretch, h * rope_w : (h + 1) * rope_w]
                    for b in range(requests)
                ],
                axis=1,
            )
            for h in range(heads)
        ],
        axis=0,
    ).astype(BF16)
    mine = lambda at: pl.ds(pl.multiple_of(at * keys, 128), keys)
    out_rows = outw_hbm.shape[0]
    load_crope = load(crope_hbm, crope_v.at[:, :, mine(c)], 0)
    load_lat = [load(lat_hbm.at[b], lat_v.at[b, mine(c)], 1 + b) for b in range(requests)]
    if outw_v.shape[1] > model:
        outw_v[:, model:] = jnp.zeros((outw_v.shape[0], outw_v.shape[1] - model), BF16)

    def late_refs(side):
        pairs = [
            (vup_hbm.at[h], vup_v.at[side, :, h * value_w : (h + 1) * value_w])
            for h in range(heads)
        ]
        cut = out_rows // 2
        return [
            *pairs,
            (outw_hbm.at[:cut], outw_v.at[side * out_rows : side * out_rows + cut, :model]),
            (outw_hbm.at[cut:], outw_v.at[side * out_rows + cut : (side + 1) * out_rows, :model]),
        ]

    def late_loads():
        return [
            pltpu.make_async_copy(src, dst, ld_sem.at[1 + requests + i])
            for i, (src, dst) in enumerate(late_refs(1))
        ]

    @pl.when(c == 1)
    def _():
        for copy in late_loads():
            copy.start()

    pl.semaphore_wait(barrier, chips)

    others, everyone = pl.ds(0, chips - 1), pl.ds(0, chips)
    group = 1 - c

    def sent(ref, sem):
        remote(ref, ref, sem, sem, partner).wait_send()

    def received(ref, sem):
        remote(ref, ref, sem, sem, partner).wait_recv()

    def queries(b, at):
        return qbuf.at[b, at] if b == 0 else qbuf.at[b, at, :, :lat_w]

    def lat_copy(b, side):
        return remote(lat_hbm.at[b], lat_v.at[b, mine(side)], kvs.at[b], kvr.at[b], partner)

    def crope_copy(side):
        return remote(
            crope_hbm, crope_v.at[:, :, mine(side)], kvs.at[requests], kvr.at[requests], partner
        )

    def late_copies():
        return [
            remote(
                src, dst, kvs.at[requests + 1 + i], kvr.at[requests + 1 + i], partner
            )
            for i, (src, dst) in enumerate(late_refs(0))
        ]

    def send_queries(b, ks):
        for k in ks:
            src = qown.at[b] if b == 0 else qown.at[b, :, :lat_w]
            remote(src, queries(b, chip), qs.at[b], qr.at[b], peer(k) * 2 + 1 - c).start()

    send_queries(0, [*far_first, 0])
    crope_copy(c).start()
    for b in range(requests):
        lat_copy(b, c).start()
    crope_copy(1 - c).wait_recv()

    @pl.when(c == 1)
    def _():
        lat_copy(0, 1 - c).wait_recv()

    for b in range(1, requests):
        send_queries(b, [*far_first, 0])
    received(queries(0, everyone), qr.at[0])

    @pl.when(c != 1)
    def _():
        lat_copy(0, 1 - c).wait_recv()

    @pl.when(c == 0)
    def _():
        for copy in late_copies()[:4]:
            copy.start()

    first_key = chip * chip_keys
    per_request = chips * block_rows
    tiles = per_request // tile
    tile_chips = tile // block_rows
    lane = lax.broadcasted_iota(jnp.int32, (tile, 128), 1)

    def attend(b, d0):
        query = qbuf[b, pl.ds(d0, tile_chips), :, :lat_w].reshape(tile, lat_w)
        rope_at = lat_w + b * rope_w
        rope = qbuf[0, pl.ds(d0, tile_chips), :, rope_at : rope_at + rope_w].reshape(tile, rope_w)
        row = lax.broadcasted_iota(jnp.int32, (tile, 1), 0) % stretch
        limit = len_s[b] + row - first_key
        peak = None
        for at in range(0, chip_keys, chunk):
            if at == keys:
                if tiles == 1 and b:
                    lat_copy(b, 1 - c).wait_recv()
            span = slice(at, at + chunk)
            begin = (at + c * keys) % chip_keys
            keyed = pl.ds(pl.multiple_of(begin, chunk), chunk)
            raw = lax.dot_general(query, lat_v[b, keyed], NT, preferred_element_type=F32)
            raw = raw + jnp.dot(rope, crope_v[b, :, keyed], preferred_element_type=F32)
            where_key = lax.broadcasted_iota(jnp.int32, (tile, chunk), 1) + begin
            raw = jnp.where(where_key <= limit, raw, masked_score)
            score_s[:, span] = raw
            high = jnp.max(raw, axis=1, keepdims=True)
            peak = high if peak is None else jnp.maximum(peak, high)
        total, pooled = None, None
        for at in range(0, chip_keys, chunk):
            span = slice(at, at + chunk)
            begin = (at + c * keys) % chip_keys
            keyed = pl.ds(pl.multiple_of(begin, chunk), chunk)
            weights = jnp.exp2((score_s[:, span] - peak) * scale2)
            part = jnp.sum(weights, axis=1, keepdims=True)
            pool = jnp.dot(weights.astype(BF16), lat_v[b, keyed], preferred_element_type=F32)
            total = part if total is None else total + part
            pooled = pool if pooled is None else pooled + pool
        stat = jnp.transpose(jnp.where(lane == 0, peak, total))
        stat_b[b, group * chips + chip, :, pl.ds(pl.multiple_of(d0 * block_rows, 128), tile)] = stat[:2]
        to = pl.ds(d0, tile_chips)
        sb[b, to] = pooled.astype(BF16).reshape(tile_chips, block_rows, lat_w)
        pool_s[b, to] = pooled.reshape(tile_chips, block_rows, lat_w)

    def pool_copy(b, k):
        return remote(
            sb.at[b, peer(k)], rb.at[b, group * chips + chip], qs.at[b], pr.at[b],
            peer(k) * 2 + 1,
        )

    for b in range(requests):
        load_lat[b].wait()
        if b == 0:
            load_crope.wait()
        if b:
            received(queries(b, everyone), qr.at[b])
        if tiles > 1 and b:
            lat_copy(b, 1 - c).wait_recv()
        if tiles == 1:
            attend(b, 0)
        else:
            def step(t, carry, b=b):
                attend(b, t * tile_chips)
                return carry
            lax.fori_loop(0, tiles, step, 0)
        sent(queries(b, everyone), qs.at[b])
        for k in far_first:
            ref = stat_b.at[b, group * chips + chip]
            remote(ref, ref, ts.at[b], tr.at[b], peer(k) * 2 + 1).start()
        for k in far_first:
            pool_copy(b, k).start()

        @pl.when(c == 0)
        def _():
            ref = stat_b.at[b, group * chips + chip]
            remote(ref, ref, ts.at[b], tr.at[b], partner).start()
            pool_copy(b, 0).start()
            if b == 0:
                for copy in late_copies()[4:]:
                    copy.start()

    def combine(b):
        received(stat_b.at[b, pl.ds(0, 2 * chips - 1)], tr.at[b])
        weight = []
        for g in range(2):
            at_chips = slice(g * chips, (g + 1) * chips)
            peaks, totals = stat_b[b, at_chips, 0, :], stat_b[b, at_chips, 1, :]
            factors = jnp.exp2((peaks - jnp.max(peaks, axis=0, keepdims=True)) * scale2)
            factors = factors / jnp.sum(factors * totals, axis=0, keepdims=True)
            factors = jnp.concatenate(
                [factors, jnp.zeros((128 - chips, per_request), F32)], axis=0
            )
            for at in range(0, per_request, 128):
                turn_s[g, at : at + 128] = jnp.transpose(factors[:, at : at + 128])
            mine = turn_s[g, pl.ds(pl.multiple_of(chip * block_rows, block_rows), block_rows)]
            lane = lax.broadcasted_iota(jnp.int32, (block_rows, 128), 1)
            weight.append([
                jnp.sum(jnp.where(lane == peer(k), mine, 0.0), axis=1, keepdims=True)
                for k in range(chips)
            ])
        received(rb.at[b, pl.ds(0, 2 * chips - 1)], pr.at[b])
        head_values = []
        for g in range(2):
            attended = 0.0
            for k in range(chips):
                if g == 0 and k == 0:
                    pooled = pool_s[b, chip]
                else:
                    pooled = rb[b, g * chips + peer(k)].astype(F32)
                attended = attended + weight[g][k] * pooled
            values = jnp.dot(attended.astype(BF16), vup_v[g], preferred_element_type=F32)
            for h in range(heads):
                head_values.append(
                    values[h * stretch : (h + 1) * stretch, h * value_w : (h + 1) * value_w]
                )
        return jnp.concatenate(head_values, axis=1).astype(BF16)

    upper = chip // (chips // 2)

    def far_owner(i):
        return (owners - 1 - i) * (1 - upper) + i * upper

    def out_copy(b, o):
        return remote(
            ob.at[b, o], orb.at[b, chip], os.at[b], orr.at[b], (base + o) * 2 + 1
        )

    def project(b, head_values):
        for i in range(owners):
            o = far_owner(i)
            at = pl.ds(pl.multiple_of(o * width, 128), width)
            piece = jnp.dot(head_values, outw_v[:, at], preferred_element_type=F32)
            opart[b, o] = piece
            ob[b, o] = piece.astype(BF16)

            @pl.when(chip != base + o)
            def _():
                out_copy(b, o).start()

    is_owner = jnp.logical_and(chip >= base, chip < base + owners)

    def fin_copy(b, o, k):
        ref = fin.at[b, o]
        return remote(ref, ref, fs.at[b], fr.at[b], peer(k) * 2 + 1)

    def relay_copy(b):
        return remote(fin.at[b], fin.at[b], gs.at[b], gr.at[b], partner)

    def reduce_out(b):
        @pl.when(is_owner)
        def _():
            o = chip - base
            received(orb.at[b, others], orr.at[b])
            summed = opart[b, o]
            for k in near_first:
                summed = summed + orb[b, peer(k)].astype(F32)
            fin[b, o] = summed.astype(BF16)
            for k in far_first:
                fin_copy(b, o, k).start()

    def by_role(wait):
        if owners > 1:
            @pl.when(is_owner)
            def _():
                wait(pl.ds(0, owners - 1))

        @pl.when(jnp.logical_not(is_owner))
        def _():
            wait(pl.ds(0, owners))

    def place():
        for o in range(owners):
            used = min(width, model - o * width)
            if used > 0:
                at = o * width
                out_ref[:, at : at + used] = jnp.concatenate(
                    [fin[b, o, :, :used].astype(F32) for b in range(requests)], axis=0
                ).astype(BF16)

    def finish_queries():
        crope_copy(c).wait_send()
        for b in range(requests):
            lat_copy(b, c).wait_send()

    @pl.when(c == 0)
    def _():
        finish_queries()
        for copy in late_copies():
            copy.wait_send()
        for b in range(requests):
            sent(stat_b.at[b, everyone], ts.at[b])
            sent(sb.at[b, everyone], qs.at[b])
        for b in range(requests):
            relay_copy(b).wait_recv()
        place()

    @pl.when(c == 1)
    def _():
        for copy in late_loads():
            copy.wait()
        for copy in late_copies()[:heads]:
            copy.wait_recv()
        for b in range(requests):
            head_values = combine(b)
            if b == 0:
                for copy in late_copies()[heads:]:
                    copy.wait_recv()
            project(b, head_values)
        finish_queries()
        for b in range(requests):
            reduce_out(b)
        for b in range(requests):
            sent(stat_b.at[b, others], ts.at[b])
            sent(sb.at[b, others], qs.at[b])
            by_role(lambda part: sent(ob.at[b, part], os.at[b]))
        for b in range(requests):
            by_role(lambda part: received(fin.at[b, part], fr.at[b]))
            relay_copy(b).start()
        place()

        @pl.when(is_owner)
        def _():
            for b in range(requests):
                sent(orb.at[b, others], fs.at[b])

        for b in range(requests):
            relay_copy(b).wait_send()


def local(
    n, query_input, query_gain, nope_weight, rope_weight, key_up, value_up, out_weight,
    cache_latent, cache_rope, cached_length,
):
    heads, _, lat_w = key_up.shape
    value_w = value_up.shape[2]
    rows = query_input.shape[0]
    requests, keys, _ = cache_latent.shape
    rope_w = rope_weight.shape[1] // heads
    stretch = rows // requests
    block_rows = heads * stretch
    model = out_weight.shape[1]
    chips = n // 2
    owners = max(1, chips // 2)
    tile = min(128, chips * block_rows)
    chunk = min(512, 2 * keys)
    width = -(-model // (128 * owners)) * 128
    vmem = pltpu.VMEM
    dma = lambda *count: pltpu.SemaphoreType.DMA(count)
    any_spec = pl.BlockSpec(memory_space=pl.ANY)
    per_block = (requests, chips, block_rows)
    return pl.pallas_call(
        functools.partial(kernel, n, tile, chunk),
        out_shape=jax.ShapeDtypeStruct((rows, model), BF16),
        in_specs=[any_spec] * 10,
        out_specs=pl.BlockSpec(memory_space=pltpu.VMEM),
        scratch_shapes=[
            vmem(query_input.shape, BF16), vmem(query_gain.shape, BF16),
            vmem(nope_weight.shape, BF16), vmem(rope_weight.shape, BF16),
            vmem(key_up.shape, BF16), vmem((2, lat_w, heads * value_w), BF16),
            vmem((2 * out_weight.shape[0], owners * width), BF16),
            vmem((requests, 2 * keys, lat_w), BF16),
            vmem((requests, rope_w, 2 * keys), BF16),
            pltpu.SMEM(cached_length.shape, jnp.int32),
            vmem((requests, block_rows, lat_w + requests * rope_w), BF16),
            vmem((*per_block, lat_w + requests * rope_w), BF16),
            vmem((tile, 2 * keys), F32),
            vmem((requests, 2 * chips, 2, chips * block_rows), F32),
            vmem((2, chips * block_rows, 128), F32), vmem((*per_block, lat_w), F32),
            vmem((*per_block, lat_w), BF16), vmem((requests, 2 * chips, block_rows, lat_w), BF16),
            vmem((requests, owners, stretch, width), F32),
            vmem((requests, owners, stretch, width), BF16),
            vmem((requests, chips, stretch, width), BF16),
            vmem((requests, owners, stretch, width), BF16),
            dma(max(6, 3 + requests + heads)), dma(requests + 3 + heads), dma(requests + 3 + heads),
            *[dma(requests)] * 11,
        ],
        compiler_params=pltpu.CompilerParams(
            collective_id=0, has_side_effects=True, vmem_limit_bytes=40 * 1024 * 1024
        ),
    )(*[
        pltpu.with_memory_space_constraint(array, pltpu.HBM)
        for array in (
            query_input, query_gain, nope_weight, rope_weight, key_up,
            value_up, out_weight, cache_latent, cache_rope, cached_length,
        )
    ])


def solution(mesh):
    placed = (
        P("groups", None),
        P(),
        P(None, "ctx"),
        P(None, "ctx"),
        P("ctx", None, None),
        P("ctx", None, None),
        P("ctx", None),
        P("groups", "ctx", None),
        P("groups", None, "ctx"),
        P("groups"),
    )
    return jax.shard_map(
        functools.partial(local, mesh.shape["ctx"]), mesh=mesh, in_specs=placed,
        out_specs=P("groups", None), check_vma=False,
    )
```

time: 32.8 us -> 32.2 us (0.982)
  Pallas kernels: 32 us -> 31.3 us
    pallas_call x1, Pallas kernels: 32 us -> 31.3 us  [local(): pl.pallas_call(functools.partial(kernel, n, tile, chunk), out_shape=jax.S...]
where the time goes in v4:
time: 32.2 us; the launch traced here: 32 us
  Pallas kernels  31.3 us (97%)
  local copies, waits for them, and re-layouts  0.69 us (2%)
    pallas_call x1, Pallas kernels, local(): pl.pallas_call(functools.partial(kernel, n, tile, chunk), out_shape=jax.S...  31.3 us
    unnamed x1, local copies, waits for them, and re-layouts  0.69 us

profile of v4, /device:TPU:0, one launch (start us, length us, event | category | flops | bytes accessed | tf_op | source)
XLA Modules:
  0.0 32.0 jit_solution(2614762386665987910)
XLA Ops:
  0.0 31.3 %shard_map.100 = bf16[16,7168]{1,0:T(8,128)(2,1)S(1)} custom-call(bf16[16,1536]{1,0:T(8,128)(2,1)} %x_hbm.1, bf16[1536]{0:T(1024)(128)(2,1)} %gain_hbm.1, bf16[1536,256]{1,0:T(8,128)(2,1)} %nope_hbm.1, bf16[1536,128]{1,0:T(8,128)(2,1)} %ropew_hbm.1, bf16[2,128,512]{2,1,0:T(8,128)(2,1)} %kup_hbm.1, bf16[2,512,128]{2,1,0:T(8,128)(2,1)} %vup_hbm.1, ...), custom_call_target="tpu_custom_call" | custom-call | tf_op jit(solution)/shard_map/pallas_call | solution.py:455
  31.3 0.7 %copy.12 = bf16[16,7168]{1,0:T(8,128)(2,1)} copy(bf16[16,7168]{1,0:T(8,128)(2,1)S(1)} %shard_map.100) | data formatting | bytes 458752

commit v5 on v4

--- a/solution.py
+++ b/solution.py
@@ -180,7 +180,7 @@
             src = qown.at[b] if b == 0 else qown.at[b, :, :lat_w]
             remote(src, queries(b, chip), qs.at[b], qr.at[b], peer(k) * 2 + 1 - c).start()
 
-    send_queries(0, [*far_first, 0])
+    send_queries(0, [0, *far_first])
     crope_copy(c).start()
     for b in range(requests):
         lat_copy(b, c).start()
@@ -268,7 +268,7 @@
                 return carry
             lax.fori_loop(0, tiles, step, 0)
         sent(queries(b, everyone), qs.at[b])
-        for k in far_first:
+        for k in near_first:
             ref = stat_b.at[b, group * chips + chip]
             remote(ref, ref, ts.at[b], tr.at[b], peer(k) * 2 + 1).start()
         for k in far_first:
@@ -446,7 +446,7 @@
     chips = n // 2
     owners = max(1, chips // 2)
     tile = min(128, chips * block_rows)
-    chunk = min(512, 2 * keys)
+    chunk = min(2048, 2 * keys)
     width = -(-model // (128 * owners)) * 128
     vmem = pltpu.VMEM
     dma = lambda *count: pltpu.SemaphoreType.DMA(count)

time: 32.2 us -> 32 us (level)
  no operation moved by 1% of the time
where the time goes in v5:
time: 32 us; the launch traced here: 31.8 us
  Pallas kernels  31.1 us (97%)
  local copies, waits for them, and re-layouts  0.69 us (2%)
    pallas_call x1, Pallas kernels, local(): pl.pallas_call(functools.partial(kernel, n, tile, chunk), out_shape=jax.S...  31.1 us
    unnamed x1, local copies, waits for them, and re-layouts  0.69 us

profile of v5, /device:TPU:0, one launch (start us, length us, event | category | flops | bytes accessed | tf_op | source)
XLA Modules:
  0.0 31.8 jit_solution(1916637556536122104)
XLA Ops:
  0.0 31.1 %shard_map.100 = bf16[16,7168]{1,0:T(8,128)(2,1)S(1)} custom-call(bf16[16,1536]{1,0:T(8,128)(2,1)} %x_hbm.1, bf16[1536]{0:T(1024)(128)(2,1)} %gain_hbm.1, bf16[1536,256]{1,0:T(8,128)(2,1)} %nope_hbm.1, bf16[1536,128]{1,0:T(8,128)(2,1)} %ropew_hbm.1, bf16[2,128,512]{2,1,0:T(8,128)(2,1)} %kup_hbm.1, bf16[2,512,128]{2,1,0:T(8,128)(2,1)} %vup_hbm.1, ...), custom_call_target="tpu_custom_call" | custom-call | tf_op jit(solution)/shard_map/pallas_call | solution.py:455
  31.1 0.7 %copy.12 = bf16[16,7168]{1,0:T(8,128)(2,1)} copy(bf16[16,7168]{1,0:T(8,128)(2,1)S(1)} %shard_map.100) | data formatting | bytes 458752
